TPU v7x, 512 devices: a whole 4x8x8 slice. The times are simulated.
512 devices in a mesh: row: 32 (over x, y_lo, core), col: 16 (over z, y_hi).
Axes of the slice: x: 4, y: 8 (y_hi: 2, y_lo: 4; y = y_hi * 4 + y_lo), z: 8, core: 2. Of those that a mesh axis runs over, the one named last changes fastest.
Arguments:
- legendre: bfloat16 [4, 128, 23, 32, 128], P(None, 'col', None, 'row'), may hold values from -6 to 6
- longitude: float32 [512], replicated, may hold values from -3.140625 to 3.140625
- obs_weight: float32 [512], replicated, may hold values from 0.1 to 1.9
- span_weight: float32 [8], replicated, may hold values from 0.3 to 3
- span_of: int32 [512], replicated, may hold values from 0 to 7
- tile_order: int32 [736], replicated, may hold values from 0 to 735, each once
- slab_start: int32 [1], replicated, may hold values from 0 to 692
- resident: float32 [23, 32, 16, 128, 128], P(None, 'row', 'col'), may hold values from -6 to 6
Outputs:
- updated: float32 [23, 32, 16, 128, 128], P(None, 'row', 'col')
Inputs may be any that keep to these rules, and one draw needn't show every extreme that they name: tile_order is a permutation of the slot positions.
All inputs are finite; a program needn't handle non-finite values.
Results may differ from a plain program's by a relative error of at most 0.00074.
Values may be sent and summed in bfloat16 or wider, within the bound.
A program may use at most 64 MiB of HBM per device.

v0:
```python
import math

import jax
import jax.numpy as jnp
from jax import lax
from jax.sharding import Mesh
from jax.sharding import PartitionSpec as P

DEGREE = 300
UNK = 90600
COL = ("col_0", "col_1")


def gathered_by_axis(array, axes, dim):
    if not axes:
        return array
    nearer = lax.all_gather(array, axes[-1], axis=dim, tiled=True)
    return gathered_by_axis(nearer, axes[:-1], dim)


def in_blocks(array, dim, count):
    before, after = (array.shape[:dim], array.shape[dim + 1 :])
    return jnp.moveaxis(array.reshape(*before, count, -1, *after), dim, 0)


def sent_and_summed(array, axis, dim):
    count = lax.axis_size(axis)
    parts = lax.all_to_all(in_blocks(array, dim, count), axis, 0, 0, tiled=True)
    return jnp.sum(parts.astype(jnp.float32), axis=0)


def padded_to(lines, count):
    spare = -len(lines) % count
    return jnp.pad(lines, [(0, spare)] + [(0, 0)] * (lines.ndim - 1))


def in_order(parts, dim):
    parts = jnp.moveaxis(parts, 0, dim)
    dims = parts.shape
    return parts.reshape(*dims[:dim], dims[dim] * dims[dim + 1], *dims[dim + 2 :])


def copy_for_each(array, axis):
    count = lax.axis_size(axis)
    return lax.all_to_all(
        jnp.broadcast_to(array[None], (count, *array.shape)), axis, 0, 0, tiled=True
    )


def collect(array, axis, dim):
    return in_order(copy_for_each(array, axis), dim)


def total_of(array, axes):
    lines = array.reshape(-1, array.shape[-1])
    own = sent_and_summed(padded_to(lines, lax.axis_size(axes)), axes, 0)
    whole = collect(own.astype(jnp.bfloat16), axes, 0)
    return whole[: len(lines)].reshape(array.shape).astype(jnp.float32)


def lookup_weights(obs_weight, span_weight, span_of):
    group_count = span_weight.shape[0]
    matches = span_of[:, None] == jnp.arange(group_count, dtype=jnp.int32)[None, :]
    factor = jnp.sum(jnp.where(matches, span_weight[None, :], 0.0), axis=1)
    return obs_weight * factor * (0.25 / math.sqrt(obs_weight.shape[0]))


def locate(tile_order, targets):
    places = jnp.arange(tile_order.shape[0], dtype=jnp.int32)
    return jnp.sum(jnp.where(tile_order[None, :] == targets[:, None], places[None, :], 0), axis=1)


def contract_rows(left_side, right_side):
    return lax.dot_general(
        left_side, right_side, (((0,), (0,)), ((), ())), preferred_element_type=jnp.float32
    )


def per_device(
    legendre, longitude, obs_weight, span_weight, span_of, tile_order, slab_start, resident
):
    block_count, shard_rows, slot_count, _, tile_size = legendre.shape
    row_count = lax.axis_size("row")
    col_count = lax.axis_size(COL)
    row_index = lax.axis_index("row")
    col_index = lax.axis_index(COL)
    block_rows = shard_rows * col_count
    order_map = tile_order.reshape(slot_count, row_count)
    own_tiles = lax.dynamic_slice_in_dim(order_map, row_index, 1, 1)[:, 0]
    unknown = own_tiles[:, None] * tile_size + jnp.arange(tile_size, dtype=jnp.int32)[None, :]
    orders = (unknown % (DEGREE + 1)).astype(jnp.float32).reshape(1, slot_count * tile_size)
    is_valid = (unknown < UNK).reshape(1, slot_count * tile_size)
    targets = slab_start[0] + jnp.arange(col_count, dtype=jnp.int32)
    positions = locate(tile_order, targets)
    target = targets[col_index]
    root_row = positions[col_index] % row_count
    root_slots = positions // row_count
    root_slot = root_slots[col_index]
    is_root = row_index == root_row
    weights = lookup_weights(obs_weight, span_weight, span_of).reshape(block_count, block_rows)
    angles = longitude.reshape(block_count, block_rows)
    in_lower = own_tiles >= target
    zero_piece = jnp.zeros((), jnp.bfloat16)
    all_values = legendre.reshape(block_count * shard_rows, slot_count * tile_size)
    own_angles = lax.dynamic_slice_in_dim(angles, col_index * shard_rows, shard_rows, 1)
    own_angles = own_angles.reshape(block_count * shard_rows)
    design_all = jnp.where(
        is_valid, all_values.astype(jnp.float32) * jnp.cos(own_angles[:, None] * orders), 0.0
    ).astype(jnp.bfloat16)
    design_all = design_all.reshape(block_count, shard_rows, slot_count * tile_size)
    gathered = gathered_by_axis(design_all, COL, 1)
    gathered = gathered.reshape(block_count * block_rows, slot_count * tile_size)
    candidate = lax.dynamic_slice_in_dim(gathered, root_slot * tile_size, tile_size, 1)
    column = total_of(jnp.where(is_root, candidate, zero_piece), "row")
    weighted = (weights.reshape(block_count * block_rows)[:, None] * column).astype(jnp.bfloat16)
    running = contract_rows(gathered, weighted)
    update = jnp.where(
        in_lower[:, None, None], running.reshape(slot_count, tile_size, tile_size), 0.0
    )
    return resident + update.reshape(resident.shape)


def solution(mesh):
    torus = Mesh(mesh.devices.reshape(mesh.shape["row"], 8, 2), ("row", "col_0", "col_1"))
    return jax.shard_map(
        per_device,
        mesh=torus,
        in_specs=(
            P(None, COL, None, "row", None),
            P(),
            P(),
            P(),
            P(),
            P(),
            P(),
            P(None, "row", COL, None, None),
        ),
        out_specs=P(None, "row", COL, None, None),
        check_vma=False,
    )
```

profile of v0, /device:TPU:1, one launch (start us, length us, event | category | flops | bytes accessed | tf_op | source)
XLA Modules:
  0.0 119.4 jit_solution(5704957825092977792)
XLA Ops:
  6.5 0.0 copy-start
  6.5 0.0 copy-start.2
  6.5 0.0 copy-start.3
  6.5 0.0 copy-start.1
  6.5 0.0 all-gather.2.cloned.1.call-start
  6.6 0.8 reshape.101
  7.4 0.2 multiply_reduce_fusion
  7.5 0.1 fusion.7
  7.6 0.1 fusion.3
  7.7 0.0 copy-done
  7.7 0.1 constant_dynamic-slice_fusion
  7.8 2.2 %fusion.2 = bf16[4,8,2944]{2,1,0:T(8,128)(2,1)S(1)} fusion(bf16[4,8,23,1,128]{4,1,3,2,0:T(8,128)(2,1)} %param.8, f32[2944]{0:T(1024)S(1)} %fusion.3, f32[4,8]{1,0:T(4,128)S(1)} %constant_dynamic-slice_fusion, pred[2944]{0:T(1024)(128)(4,1)S(1)} %fusion.7), kind=kLoop, calls=%fused_computation.4 | loop fusion | flops 471040 | bytes 391680 | tf_op jit(solution)/shard_map/convert_element_type | solution.py:109
  10.1 14.5 %all_gather.6 = bf16[4,16,2944]{2,1,0:T(8,128)(2,1)} all-gather(bf16[4,8,2944]{2,1,0:T(8,128)(2,1)S(1)} %fusion.2), channel_id=1, replica_groups=mesh['row'=32,'col_0'=8,'col_1'=2] {'col_1'}, dimensions={1}, use_global_device_ids=true | all-gather | bytes 565248 | tf_op jit(solution)/shard_map/all_gather | solution.py:17
  24.6 0.0 all-gather.2.cloned.1.call-update
  25.3 0.9 select_reduce_fusion
  26.1 0.6 dynamic_slice.21
  28.7 0.6 dynamic_slice.22
  29.9 47.4 %all-gather.2.cloned.1.call-done = bf16[4,128,2944]{2,1,0:T(8,128)(2,1)} async-done(((bf16[4,16,2944]{2,1,0:T(8,128)(2,1)}), bf16[4,128,2944]{2,1,0:T(8,128)(2,1)}) %all-gather.2.cloned.1.call-update) | async-done | bytes 3014672 | tf_op jit(solution)/shard_map/all_gather | solution.py:17
  77.4 0.9 dynamic-slice_select_fusion
  78.3 17.2 %all_to_all.10 = bf16[32,16,128]{2,1,0:T(8,128)(2,1)S(1)} all-to-all(bf16[32,16,128]{2,1,0:T(8,128)(2,1)S(1)} %bitcast.44), channel_id=1, replica_groups=mesh['row'=32,'col_0'=8,'col_1'=2] {'row'}, dimensions={0} | all-to-all | bytes 262144 | tf_op jit(solution)/shard_map/all_to_all | solution.py:28
  95.5 0.7 broadcast_in_dim.74
  96.2 3.9 %all-to-all-start.1 = ((bf16[32,16,128]{2,1,0:T(8,128)(2,1)}), bf16[32,16,128]{2,1,0:T(8,128)(2,1)S(1)}, u32[]{:S(2)}, u32[]{:S(2)}) async-start(bf16[32,16,128]{2,1,0:T(8,128)(2,1)} %broadcast_in_dim.74), calls=%async_computation.1 | async-start | bytes 262144 | tf_op jit(solution)/shard_map/all_to_all | solution.py:45
  100.1 0.0 copy-done.2
  100.1 0.0 copy-done.3
  100.1 0.1 select_reduce_fusion.1
  100.2 0.6 dynamic_slice.19
  100.9 0.0 copy-done.1
  100.9 0.1 mul.63
  100.9 0.8 compare_reduce_fusion
  101.8 3.4 %copy.17 = bf16[2944,512]{1,0:T(8,128)(2,1)S(1)} copy(bf16[2944,512]{0,1:T(8,128)(2,1)} %bitcast.42) | data formatting | bytes 6029312 | tf_op jit(solution)/shard_map/dot_general | solution.py:74
  105.2 3.7 %all-to-all-done.1 = bf16[32,16,128]{2,1,0:T(8,128)(2,1)S(1)} async-done(((bf16[32,16,128]{2,1,0:T(8,128)(2,1)}), bf16[32,16,128]{2,1,0:T(8,128)(2,1)S(1)}, u32[]{:S(2)}, u32[]{:S(2)}) %all-to-all-start.1) | async-done | bytes 131104 | tf_op jit(solution)/shard_map/all_to_all | solution.py:45
  108.9 0.1 multiply_convert_fusion
  109.0 3.5 %fusion = f32[23,1,1,128,128]{4,3,2,1,0:T(8,128)} fusion(f32[23,1,1,128,128]{4,3,2,1,0:T(8,128)} %param.15, bf16[23,128,512]{2,1,0:T(8,128)(2,1)S(1)} %bitcast.40, bf16[512,128,1]{1,0,2:T(8,128)(2,1)S(1)} %bitcast.43, pred[23]{0:T(512)(128)(4,1)S(1)} %compare_reduce_fusion), kind=kOutput, calls=%fused_computation.1 | convolution fusion | flops 386629632 | bytes 6160407 | tf_op jit(solution)/shard_map/dot_general | solution.py:74
  (4 shorter events, 0.1 us)
Async XLA Ops:
  6.5 1.2 copy-start
  6.5 93.6 %copy-start.2 = (s32[512]{0:T(512)S(1)}, s32[512]{0:T(512)}, u32[]{:S(2)}) copy-start(s32[512]{0:T(512)} %param.12) | copy-start | bytes 6148
  6.5 93.6 %copy-start.3 = (f32[8]{0:T(128)S(1)}, f32[8]{0:T(128)}, u32[]{:S(2)}) copy-start(f32[8]{0:T(128)} %param.11) | copy-start | bytes 100
  6.5 94.3 %copy-start.1 = (f32[512]{0:T(512)S(1)}, f32[512]{0:T(512)}, u32[]{:S(2)}) copy-start(f32[512]{0:T(512)} %param.10) | copy-start | bytes 6148
  6.5 70.8 %all-gather.2.cloned.1.call-start = ((), (), s32[]{:S(2)}) async-start(), calls=%async_computation.2 | async-start | bytes 3391488 | tf_op jit(solution)/shard_map/all_gather | solution.py:17
  96.2 12.7 %all-to-all-start.1 = ((bf16[32,16,128]{2,1,0:T(8,128)(2,1)}), bf16[32,16,128]{2,1,0:T(8,128)(2,1)S(1)}, u32[]{:S(2)}, u32[]{:S(2)}) async-start(bf16[32,16,128]{2,1,0:T(8,128)(2,1)} %broadcast_in_dim.74), calls=%async_computation.1 | async-start | bytes 262144 | tf_op jit(solution)/shard_map/all_to_all | solution.py:45
Sparse Core Ops, SparseCore 0:
  24.7 52.6 all-gather.1
where the time goes:
time: 120 us; the launch traced here: 119 us
  waiting for transfers between devices  51.2 us (43%)
  blocking collectives  31.7 us (26%)
  between operations  16.8 us (14%)
  local copies, waits for them, and re-layouts  6.84 us (6%)
  other arithmetic  5.48 us (5%)
  starting transfers between devices  3.94 us (3%)
  matrix products  3.53 us (3%)
    all_gather x1, waiting for transfers between devices, gathered_by_axis(): nearer = lax.all_gather(array, axes[-1], axis=dim, tiled=True)  47.4 us
    all_to_all x1, blocking collectives, sent_and_summed(): parts = lax.all_to_all(in_blocks(array, dim, count), axis, 0, 0, tiled=True)  17.2 us
    all_gather x1, blocking collectives, gathered_by_axis(): nearer = lax.all_gather(array, axes[-1], axis=dim, tiled=True)  14.5 us
    all_to_all x1, starting transfers between devices, copy_for_each(): lax.all_to_all(jnp.broadcast_to(array[None], (count, *array.shape)), axis...  3.91 us
    all_to_all x1, waiting for transfers between devices, copy_for_each(): lax.all_to_all(jnp.broadcast_to(array[None], (count, *array.shape)), axis...  3.73 us
    dot_general x1, matrix products, contract_rows(): lax.dot_general(left_side, right_side, (((0,), (0,)), ((), ())), preferre...  3.53 us
    dot_general x1, local copies, waits for them, and re-layouts, contract_rows(): lax.dot_general(left_side, right_side, (((0,), (0,)), ((), ())), preferre...  3.42 us
  transfers between devices with their start and end apart: 2, of which 2 were waited for; matrix products, arithmetic and copies ran while one was open for 6% of the time, Pallas kernels for 0%

commit v1 on v0

v1 whole, which is shorter than its diff:
```python
import functools
import math

import jax
import jax.numpy as jnp
from jax import lax
from jax.experimental import pallas as pl
from jax.experimental.pallas import tpu as pltpu
from jax.sharding import Mesh
from jax.sharding import PartitionSpec as P

DEGREE = 300
UNK = 90600
MESH = pl.DeviceIdType.MESH
NX, NYL, NCORE, NZ, NYH = 4, 4, 2, 8, 2
NROW = NX * NYL * NCORE
NCOL = NZ * NYH
SLOTS = 23
TILE = 128
OBS = 512
SHARD = OBS // NCOL
CHUNKS = ((0, 6), (6, 6), (12, 6), (18, 5))


def ring_hops(chunk):
    return (4, 3) if chunk % 2 == 0 else (3, 4)


def kernel(
    leg,
    lon,
    obs_w,
    span_w,
    span_of,
    order,
    slab,
    prod,
    table,
    own,
    gath,
    pair,
    sendy,
    masked,
    parts,
    column,
    weighted,
    wcol,
    ring_send,
    ring_recv,
    y_send,
    y_recv,
    c_send,
    c_recv,
):
    x, yl, core = lax.axis_index("x"), lax.axis_index("yl"), lax.axis_index("core")
    z, yh = lax.axis_index("z"), lax.axis_index("yh")
    row = (x * NYL + yl) * NCORE + core
    mine = z * NYH + yh
    other = 1 - yh

    def row_id(k):
        return {"x": k // (NYL * NCORE), "yl": (k // NCORE) % NYL, "core": k % NCORE}

    barrier = pltpu.get_barrier_semaphore()

    def hello_row(i, c):
        pl.semaphore_signal(barrier, inc=1, device_id=row_id((row + i) % NROW), device_id_type=MESH)
        return c

    def hello_z(i, c):
        pl.semaphore_signal(barrier, inc=1, device_id={"z": (z + i) % NZ}, device_id_type=MESH)
        return c

    pl.semaphore_signal(barrier, inc=1, device_id={"yh": other}, device_id_type=MESH)
    lax.fori_loop(1, NZ, hello_z, 0)
    lax.fori_loop(1, NROW, hello_row, 0)

    sub = lax.broadcasted_iota(jnp.int32, (8, TILE), 0)
    lane = lax.broadcasted_iota(jnp.int32, (8, TILE), 1)
    for b in range(4):
        own_lon = jnp.zeros((8, TILE), jnp.float32)
        for j in range(8):
            own_lon = jnp.where(sub == j, lon[b * TILE + mine * 8 + j], own_lon)
        for a in range(4):
            k = lane + a * TILE
            m = jnp.where(k > DEGREE, k - (DEGREE + 1), k).astype(jnp.float32)
            table[a, pl.ds(b * 8, 8), :] = jnp.cos(own_lon * m)

    lane32 = lax.broadcasted_iota(jnp.int32, (SHARD, TILE), 1)
    tiles = []
    for s in range(SLOTS):
        t = order[s * NROW + row]
        tiles.append(t)
        whole = (t * 111477) >> 18
        start = t * TILE - whole * (DEGREE + 1)
        a0 = start // TILE
        shift = start - a0 * TILE
        back = (TILE - shift) % TILE
        low = pltpu.roll(table[a0], back, 1)
        high = pltpu.roll(table[a0 + 1], back, 1)
        cosine = jnp.where(lane32 < TILE - shift, low, high)
        values = jnp.concatenate([leg[b, s].astype(jnp.float32) for b in range(4)], axis=0)
        value = jnp.where(lane32 < UNK - t * TILE, values * cosine, 0.0)
        own[s] = value.astype(jnp.bfloat16)
        gath[mine, s] = own[s]

    base = slab[0]
    for q in range(NCOL):
        at = jnp.int32(0)
        found = jnp.int32(0)
        for s in range(SLOTS):
            hit = tiles[s] == base + q
            at = jnp.where(hit, s, at)
            found = jnp.where(hit, 1, found)
        got = own[at].astype(jnp.float32)
        got = jnp.where(found == 1, got, 0.0).astype(jnp.bfloat16)
        cand = got.reshape(2, 16, TILE)
        zq, yq = q // NYH, q % NYH
        sendy[yq, zq] = cand

    pl.semaphore_wait(barrier, 1 + (NZ - 1) + (NROW - 1))

    def ring(direction, which, hop, chunk):
        s0, n = CHUNKS[chunk]
        sign = 1 if direction == 0 else -1
        src_z = (z - sign * (hop - 1) + NZ) % NZ
        src_y = yh if which == 0 else other
        ref = gath.at[src_z * NYH + src_y, pl.ds(s0, n)]
        return pltpu.make_async_remote_copy(
            src_ref=own.at[pl.ds(s0, n)] if which == 0 and hop == 1 else ref,
            dst_ref=ref,
            send_sem=ring_send.at[direction, which, hop - 1, chunk],
            recv_sem=ring_recv.at[direction, which, hop - 1, chunk],
            device_id={"z": (z + sign + NZ) % NZ},
            device_id_type=MESH,
        )

    def ring_arrival(direction, which, hop, chunk):
        s0, n = CHUNKS[chunk]
        sign = 1 if direction == 0 else -1
        src_z = (z - sign * hop + NZ) % NZ
        src_y = yh if which == 0 else other
        ref = gath.at[src_z * NYH + src_y, pl.ds(s0, n)]
        return pltpu.make_async_remote_copy(
            src_ref=ref,
            dst_ref=ref,
            send_sem=ring_send.at[direction, which, hop - 1, chunk],
            recv_sem=ring_recv.at[direction, which, hop - 1, chunk],
            device_id={"z": (z + sign + NZ) % NZ},
            device_id_type=MESH,
        )

    started = []

    def go(copy):
        copy.start()
        started.append(copy)

    def across(chunk):
        s0, n = CHUNKS[chunk]
        return pltpu.make_async_remote_copy(
            src_ref=own.at[pl.ds(s0, n)],
            dst_ref=gath.at[mine, pl.ds(s0, n)],
            send_sem=y_send.at[chunk],
            recv_sem=y_recv.at[chunk],
            device_id={"yh": other},
            device_id_type=MESH,
        )

    def across_arrival(chunk):
        s0, n = CHUNKS[chunk]
        ref = gath.at[z * NYH + other, pl.ds(s0, n)]
        return pltpu.make_async_remote_copy(
            src_ref=ref,
            dst_ref=ref,
            send_sem=y_send.at[chunk],
            recv_sem=y_recv.at[chunk],
            device_id={"yh": other},
            device_id_type=MESH,
        )

    chunks = range(len(CHUNKS))
    swap = pltpu.make_async_remote_copy(
        src_ref=sendy.at[other],
        dst_ref=pair,
        send_sem=c_send.at[0],
        recv_sem=c_recv.at[0],
        device_id={"yh": other},
        device_id_type=MESH,
    )
    go(swap)
    for g in chunks:
        go(ring(0, 0, 1, g))
        go(ring(1, 0, 1, g))
        go(across(g))

    def ring_round(which, hop):
        for g in chunks:
            for direction in (0, 1):
                last = ring_hops(g)[direction]
                if hop <= last:
                    ring_arrival(direction, which, hop, g).wait_recv()
                if hop < last:
                    go(ring(direction, which, hop + 1, g))

    ring_round(0, 1)

    swap_in = pltpu.make_async_remote_copy(
        src_ref=sendy.at[other],
        dst_ref=pair,
        send_sem=c_send.at[0],
        recv_sem=c_recv.at[0],
        device_id={"yh": other},
        device_id_type=MESH,
    )
    swap_in.wait_recv()

    def z_send(i, c):
        peer = (z + i) % NZ
        for half, source in ((yh, sendy.at[yh, peer]), (other, pair.at[peer])):
            pltpu.make_async_remote_copy(
                src_ref=source,
                dst_ref=masked.at[pl.ds((z * NYH + half) * 2, 2)],
                send_sem=c_send.at[1],
                recv_sem=c_recv.at[1],
                device_id={"z": peer},
                device_id_type=MESH,
            ).start()
        return c

    lax.fori_loop(1, NZ, z_send, 0)
    masked[pl.ds((z * NYH + yh) * 2, 2)] = sendy[yh, z]
    masked[pl.ds((z * NYH + other) * 2, 2)] = pair[z]

    ring_round(0, 2)

    z_bytes = masked.at[pl.ds(0, 4 * (NZ - 1))]
    pltpu.make_async_copy(z_bytes, z_bytes, c_recv.at[1]).wait()
    pltpu.make_async_copy(z_bytes, z_bytes, c_send.at[1]).wait()

    def scatter(i, c):
        k = (row + i) % NROW
        pltpu.make_async_remote_copy(
            src_ref=masked.at[k],
            dst_ref=parts.at[row],
            send_sem=c_send.at[2],
            recv_sem=c_recv.at[2],
            device_id=row_id(k),
            device_id_type=MESH,
        ).start()
        return c

    lax.fori_loop(1, NROW, scatter, 0)
    parts[row] = masked[row]

    weights = jnp.zeros((4, TILE), jnp.float32)
    for g in range(8):
        weights = jnp.where(span_of[...] == g, span_w[g], weights)
    weights = obs_w[...] * weights * (0.25 / math.sqrt(OBS))
    for b in range(4):
        wide = jnp.broadcast_to(weights[b : b + 1, :], (TILE, TILE))
        wcol[:, b] = jnp.transpose(wide).reshape(NCOL, 8, TILE)

    ring_round(0, 3)

    p_bytes = parts.at[pl.ds(0, NROW - 1)]
    pltpu.make_async_copy(p_bytes, p_bytes, c_recv.at[2]).wait()
    pltpu.make_async_copy(p_bytes, p_bytes, c_send.at[2]).wait()
    total = parts[0].astype(jnp.float32)
    for k in range(1, NROW):
        total = total + parts[k].astype(jnp.float32)
    column[row] = total.astype(jnp.bfloat16)

    for g in chunks:
        across_arrival(g).wait_recv()
        go(ring(0, 1, 1, g))
        go(ring(1, 1, 1, g))

    def spread(i, c):
        k = (row + i) % NROW
        pltpu.make_async_remote_copy(
            src_ref=column.at[row],
            dst_ref=column.at[row],
            send_sem=c_send.at[3],
            recv_sem=c_recv.at[3],
            device_id=row_id(k),
            device_id_type=MESH,
        ).start()
        return c

    lax.fori_loop(1, NROW, spread, 0)

    ring_round(0, 4)
    ring_round(1, 1)
    ring_round(1, 2)

    a_bytes = column.at[pl.ds(0, NROW - 1)]
    pltpu.make_async_copy(a_bytes, a_bytes, c_recv.at[3]).wait()
    pltpu.make_async_copy(a_bytes, a_bytes, c_send.at[3]).wait()
    for c in range(NCOL):
        col = column[pl.ds(2 * c, 2)].reshape(SHARD, TILE).astype(jnp.float32)
        weighted[pl.ds(c * SHARD, SHARD)] = (col * wcol[c].reshape(SHARD, TILE)).astype(jnp.bfloat16)

    ring_round(1, 3)

    target = base + mine
    for g in chunks:
        direction = 0 if ring_hops(g)[0] == 4 else 1
        ring_arrival(direction, 1, 4, g).wait_recv()
        s0, n = CHUNKS[g]
        for s in range(s0, s0 + n):
            left = gath[:, s].reshape(OBS, TILE)
            product = lax.dot_general(
                left, weighted[...], (((0,), (0,)), ((), ())), preferred_element_type=jnp.float32
            )
            prod[s] = jnp.where(tiles[s] >= target, product, 0.0)
    for copy in started:
        copy.wait_send()


def per_device(
    legendre, longitude, obs_weight, span_weight, span_of, tile_order, slab_start, resident
):
    leg = legendre.reshape(4, 8, SLOTS, TILE).transpose(0, 2, 1, 3)
    smem = pl.BlockSpec(memory_space=pltpu.SMEM)
    vmem = pl.BlockSpec(memory_space=pltpu.VMEM)
    bf16, f32 = jnp.bfloat16, jnp.float32
    dma = pltpu.SemaphoreType.DMA
    product = pl.pallas_call(
        kernel,
        out_shape=jax.ShapeDtypeStruct((SLOTS, TILE, TILE), f32),
        in_specs=[vmem, smem, vmem, smem, vmem, smem, smem],
        out_specs=vmem,
        scratch_shapes=[
            pltpu.VMEM((4, SHARD, TILE), f32),
            pltpu.VMEM((SLOTS, SHARD, TILE), bf16),
            pltpu.VMEM((NCOL, SLOTS, SHARD, TILE), bf16),
            pltpu.VMEM((NZ, 2, 16, TILE), bf16),
            pltpu.VMEM((NYH, NZ, 2, 16, TILE), bf16),
            pltpu.VMEM((NROW, 16, TILE), bf16),
            pltpu.VMEM((NROW, 16, TILE), bf16),
            pltpu.VMEM((NROW, 16, TILE), bf16),
            pltpu.VMEM((OBS, TILE), bf16),
            pltpu.VMEM((NCOL, 4, 8, TILE), f32),
            dma((2, 2, 4, len(CHUNKS))),
            dma((2, 2, 4, len(CHUNKS))),
            dma((len(CHUNKS),)),
            dma((len(CHUNKS),)),
            dma((4,)),
            dma((4,)),
        ],
        compiler_params=pltpu.CompilerParams(
            collective_id=0, has_side_effects=True, vmem_limit_bytes=24 * 1024 * 1024
        ),
    )(
        leg,
        longitude,
        obs_weight.reshape(4, TILE),
        span_weight,
        span_of.reshape(4, TILE),
        tile_order,
        slab_start,
    )
    return resident + product.reshape(resident.shape)


def solution(mesh):
    torus = Mesh(
        mesh.devices.reshape(NX, NYL, NCORE, NZ, NYH), ("x", "yl", "core", "z", "yh")
    )
    rows, cols = ("x", "yl", "core"), ("z", "yh")
    return jax.shard_map(
        per_device,
        mesh=torus,
        in_specs=(
            P(None, cols, None, rows, None),
            P(),
            P(),
            P(),
            P(),
            P(),
            P(),
            P(None, rows, cols, None, None),
        ),
        out_specs=P(None, rows, cols, None, None),
        check_vma=False,
    )
```

time: 120 us -> 60.8 us (0.51)
  Pallas kernels: 0 us -> 54.3 us
  waiting for transfers between devices: 51.2 us -> 0 us
  blocking collectives: 31.7 us -> 0 us
  between operations: 16.8 us -> 0.68 us
  other arithmetic: 5.48 us -> 1.29 us
  starting transfers between devices: 3.94 us -> 0 us
  matrix products: 3.53 us -> 0 us
  local copies, waits for them, and re-layouts: 6.84 us -> 4.31 us
    pallas_call x0 -> x1, Pallas kernels: none -> 54.3 us  [per_device(): pl.pallas_call(kernel, out_shape=jax.ShapeDtypeStruct((SLOTS, TILE, TILE)...]
    all_gather x1 -> x0, waiting for transfers between devices: 47.4 us -> none  [gathered_by_axis(): nearer = lax.all_gather(array, axes[-1], axis=dim, tiled=True)]
    all_to_all x1 -> x0, blocking collectives: 17.2 us -> none  [sent_and_summed(): parts = lax.all_to_all(in_blocks(array, dim, count), axis, 0, 0, tiled=True)]
    all_gather x1 -> x0, blocking collectives: 14.5 us -> none  [gathered_by_axis(): nearer = lax.all_gather(array, axes[-1], axis=dim, tiled=True)]
    unnamed x8 -> x14, local copies, waits for them, and re-layouts: 0.02 us -> 4.31 us
    all_to_all x1 -> x0, starting transfers between devices: 3.91 us -> none  [copy_for_each(): lax.all_to_all(jnp.broadcast_to(array[None], (count, *array.shape)), axis...]
    all_to_all x1 -> x0, waiting for transfers between devices: 3.73 us -> none  [copy_for_each(): lax.all_to_all(jnp.broadcast_to(array[None], (count, *array.shape)), axis...]
    dot_general x1 -> x0, matrix products: 3.53 us -> none  [contract_rows(): lax.dot_general(left_side, right_side, (((0,), (0,)), ((), ())), preferre...]
  transfers between devices with their start and end apart: 2 -> 0, of which waited for: 2 -> 0; matrix products, arithmetic and copies ran while one was open for 6% -> 0% of each run, Pallas kernels for 0% -> 0%
where the time goes in v1:
time: 60.8 us; the launch traced here: 60.6 us
  Pallas kernels  54.3 us (89%)
  local copies, waits for them, and re-layouts  4.31 us (7%)
  other arithmetic  1.29 us (2%)
  between operations  0.68 us (1%)
    pallas_call x1, Pallas kernels, per_device(): pl.pallas_call(kernel, out_shape=jax.ShapeDtypeStruct((SLOTS, TILE, TILE)...  54.3 us
    unnamed x14, local copies, waits for them, and re-layouts  4.31 us
    add x1, other arithmetic, per_device(): return resident + product.reshape(resident.shape)  1.29 us

profile of v1, /device:TPU:1, one launch (start us, length us, event | category | flops | bytes accessed | tf_op | source)
XLA Modules:
  0.0 60.6 jit_solution(14293590996769413415)
XLA Ops:
  0.7 0.0 copy-start
  0.7 0.9 %copy-done = bf16[4,8,23,1,128]{4,1,3,2,0:T(8,128)(2,1)S(1)} copy-done((bf16[4,8,23,1,128]{4,1,3,2,0:T(8,128)(2,1)S(1)}, bf16[4,8,23,1,128]{4,1,3,2,0:T(8,128)(2,1)}, u32[]{:S(2)}) %copy-start) | copy-done | bytes 188440
  1.6 0.0 copy-start.1
  1.6 0.7 %copy-done.1 = s32[736]{0:T(1024)S(1)} copy-done((s32[736]{0:T(1024)S(1)}, s32[736]{0:T(1024)}, u32[]{:S(2)}) %copy-start.1) | copy-done | bytes 2968
  2.3 0.0 copy-start.2
  2.3 0.7 %copy-done.2 = f32[512]{0:T(512)S(1)} copy-done((f32[512]{0:T(512)S(1)}, f32[512]{0:T(512)}, u32[]{:S(2)}) %copy-start.2) | copy-done | bytes 2072
  2.9 0.0 copy-start.3
  2.9 0.7 %copy-done.3 = f32[512]{0:T(512)S(1)} copy-done((f32[512]{0:T(512)S(1)}, f32[512]{0:T(512)}, u32[]{:S(2)}) %copy-start.3) | copy-done | bytes 2072
  3.6 0.0 copy-start.4
  3.6 0.7 %copy-done.4 = s32[512]{0:T(512)S(1)} copy-done((s32[512]{0:T(512)S(1)}, s32[512]{0:T(512)}, u32[]{:S(2)}) %copy-start.4) | copy-done | bytes 2072
  4.3 0.0 copy-start.5
  4.3 0.7 %copy-done.5 = f32[8]{0:T(128)S(1)} copy-done((f32[8]{0:T(128)S(1)}, f32[8]{0:T(128)}, u32[]{:S(2)}) %copy-start.5) | copy-done | bytes 56
  5.0 0.0 copy-start.6
  5.0 54.3 %shard_map.82 = f32[23,128,128]{2,1,0:T(8,128)S(1)} custom-call(bf16[4,23,8,128]{3,2,1,0:T(8,128)(2,1)S(1)} %bitcast.13, f32[512]{0:T(512)S(1)} %copy-done.2, f32[4,128]{1,0:T(4,128)S(1)} %bitcast.14, f32[8]{0:T(128)S(1)} %copy-done.5, s32[4,128]{1,0:T(4,128)S(1)} %bitcast.15, s32[736]{0:T(1024)S(1)} %copy-done.1, s32[1]{0:T(128)S(6)} %copy.11.slab), custom_call_target="tpu_custom_call" | custom-call | tf_op jit(solution)/shard_map/pallas_call | solution.py:329
  59.3 0.0 copy-done.6
  59.3 1.3 %fusion = f32[23,1,1,128,128]{4,3,2,1,0:T(8,128)} fusion(f32[23,128,128]{2,1,0:T(8,128)S(1)} %shard_map.82, f32[23,1,1,128,128]{4,3,2,1,0:T(8,128)S(1)} %copy-done.6), kind=kLoop, calls=%fused_computation.1 | loop fusion | flops 376832 | bytes 4521984 | tf_op jit(solution)/shard_map/add | solution.py:364
Async XLA Ops:
  0.7 0.9 %copy-start = (bf16[4,8,23,1,128]{4,1,3,2,0:T(8,128)(2,1)S(1)}, bf16[4,8,23,1,128]{4,1,3,2,0:T(8,128)(2,1)}, u32[]{:S(2)}) copy-start(bf16[4,8,23,1,128]{4,1,3,2,0:T(8,128)(2,1)} %param.8) | copy-start | bytes 565252
  1.6 0.7 %copy-start.1 = (s32[736]{0:T(1024)S(1)}, s32[736]{0:T(1024)}, u32[]{:S(2)}) copy-start(s32[736]{0:T(1024)} %order.1) | copy-start | bytes 8836
  2.3 0.7 %copy-start.2 = (f32[512]{0:T(512)S(1)}, f32[512]{0:T(512)}, u32[]{:S(2)}) copy-start(f32[512]{0:T(512)} %lon.1) | copy-start | bytes 6148
  2.9 0.7 %copy-start.3 = (f32[512]{0:T(512)S(1)}, f32[512]{0:T(512)}, u32[]{:S(2)}) copy-start(f32[512]{0:T(512)} %param.10) | copy-start | bytes 6148
  3.6 0.7 %copy-start.4 = (s32[512]{0:T(512)S(1)}, s32[512]{0:T(512)}, u32[]{:S(2)}) copy-start(s32[512]{0:T(512)} %param.12) | copy-start | bytes 6148
  4.3 0.7 %copy-start.5 = (f32[8]{0:T(128)S(1)}, f32[8]{0:T(128)}, u32[]{:S(2)}) copy-start(f32[8]{0:T(128)} %span_w.1) | copy-start | bytes 100
  5.0 54.3 %copy-start.6 = (f32[23,1,1,128,128]{4,3,2,1,0:T(8,128)S(1)}, f32[23,1,1,128,128]{4,3,2,1,0:T(8,128)}, u32[]{:S(2)}) copy-start(f32[23,1,1,128,128]{4,3,2,1,0:T(8,128)} %param.15) | copy-start | bytes 4521988

commit v2 on v0

v2 whole, which is shorter than its diff:
```python
import functools
import math

import jax
import jax.numpy as jnp
from jax import lax
from jax.experimental import pallas as pl
from jax.experimental.pallas import tpu as pltpu
from jax.sharding import Mesh
from jax.sharding import PartitionSpec as P

DEGREE = 300
UNK = 90600
TILES = 708
MESH = pl.DeviceIdType.MESH
NX, NYL, NCORE, NZ, NYH = 4, 4, 2, 8, 2
NROW = NX * NYL * NCORE
NCOL = NZ * NYH
SLOTS = 23
TILE = 128
OBS = 512
SHARD = OBS // NCOL
SIZES = (10, 14, 17, 20, 23)


def chunks_of(slots):
    count = min(4, slots)
    edges = [slots * i // count for i in range(count + 1)]
    return tuple((a, b - a) for a, b in zip(edges[:-1], edges[1:]))


def hops(which, chunk):
    if which == 1:
        return (3, 3)
    return (4, 3) if chunk % 2 == 0 else (3, 4)


def plan_of(slots):
    if slots > 14:
        return (
            (0, 1), (0, 2), "added", (0, 3), "others", (0, 4), "spread", (1, 1), (1, 2), "in",
        )
    return (
        (0, 1), (0, 2), "added", "others", (0, 3), (0, 4), (1, 1), "spread", (1, 2), "in",
    )


def kernel(
    slots,
    leg_in,
    lon_in,
    obs_w_in,
    span_w_in,
    span_of_in,
    order_in,
    slab_in,
    prod,
    leg,
    lon,
    obs_w,
    span_w,
    span_of,
    order,
    slab,
    table,
    own,
    gath,
    masked,
    parts,
    summed,
    column,
    weighted,
    wcol,
    packed,
    in_sem,
    ring_send,
    ring_recv,
    y_send,
    y_recv,
    c_send,
    c_recv,
):
    chunks = chunks_of(slots)
    compact = slots < SLOTS
    x, yl, core = lax.axis_index("x"), lax.axis_index("yl"), lax.axis_index("core")
    z, yh = lax.axis_index("z"), lax.axis_index("yh")
    row = (x * NYL + yl) * NCORE + core
    mine = z * NYH + yh
    other = 1 - yh
    half = row % 2
    facing_z, facing_y = (row // 4 - z + NZ) % NZ, (row // 2 + yh) % NYH
    away = (facing_z != z) | (facing_y != yh)

    def row_id(k):
        return {"x": k // (NYL * NCORE), "yl": (k // NCORE) % NYL, "core": k % NCORE}

    facing = {"z": facing_z, "yh": facing_y}

    def met(k):
        return ((k // 4 - z + NZ) % NZ) * NYH + (k // 2 + yh) % NYH

    inputs = []
    for i, (source, to) in enumerate(
        (
            (order_in, order),
            (slab_in, slab),
            (lon_in, lon),
            (leg_in, leg),
            (obs_w_in, obs_w),
            (span_w_in, span_w),
            (span_of_in, span_of),
        )
    ):
        copy = pltpu.make_async_copy(source, to, in_sem.at[i])
        copy.start()
        inputs.append(copy)

    barrier = pltpu.get_barrier_semaphore()

    def hello(to):
        pl.semaphore_signal(barrier, inc=1, device_id=to, device_id_type=MESH)

    def hello_row(i, c):
        hello(row_id((row + i) % NROW))
        return c

    hello({"z": (z + 1) % NZ})
    hello({"z": (z + NZ - 1) % NZ})
    hello({"yh": other})

    @pl.when(away)
    def _():
        hello(facing)

    lax.fori_loop(1, NROW, hello_row, 0)

    for copy in inputs[:3]:
        copy.wait()
    base = slab[0]
    tiles = [order[s * NROW + row] for s in range(SLOTS)]
    if compact:
        index = [jnp.int32(0)] * slots
        place, at = [], jnp.int32(0)
        for s in range(SLOTS):
            need = (tiles[s] >= base) & (tiles[s] < TILES)
            hit = jnp.where(need, at, -1)
            for k in range(min(s + 1, slots)):
                index[k] = jnp.where(hit == k, s, index[k])
            place.append(hit)
            at = at + jnp.where(need, 1, 0)
        held = [order[i * NROW + row] for i in index]
    else:
        index, held = list(range(SLOTS)), tiles

    sub = lax.broadcasted_iota(jnp.int32, (8, TILE), 0)
    lane = lax.broadcasted_iota(jnp.int32, (8, TILE), 1)
    for b in range(4):
        own_lon = jnp.zeros((8, TILE), jnp.float32)
        for j in range(8):
            own_lon = jnp.where(sub == j, lon[b * TILE + mine * 8 + j], own_lon)
        for a in range(4):
            k = lane + a * TILE
            m = jnp.where(k > DEGREE, k - (DEGREE + 1), k).astype(jnp.float32)
            table[a, pl.ds(b * 8, 8), :] = jnp.cos(own_lon * m)
    for copy in inputs[3:]:
        copy.wait()

    lane32 = lax.broadcasted_iota(jnp.int32, (SHARD, TILE), 1)

    def design(chunk):
        s0, n = chunks[chunk]
        for s in range(s0, s0 + n):
            t = held[s]
            start = t * TILE - ((t * 111477) >> 18) * (DEGREE + 1)
            a0 = start // TILE
            shift = start - a0 * TILE
            back = (TILE - shift) % TILE
            low = pltpu.roll(table[a0], back, 1)
            high = pltpu.roll(table[a0 + 1], back, 1)
            cosine = jnp.where(lane32 < TILE - shift, low, high)
            values = jnp.concatenate(
                [leg[b, index[s]].astype(jnp.float32) for b in range(4)], axis=0
            )
            value = jnp.where(lane32 < UNK - t * TILE, values * cosine, 0.0)
            own[s] = value.astype(jnp.bfloat16)

    started = []

    def go(copy):
        copy.start()
        started.append(copy)

    def ring(direction, which, hop, chunk, arriving=False):
        s0, n = chunks[chunk]
        sign = 1 if direction == 0 else -1
        src_z = (z - sign * (hop if arriving else hop - 1) + NZ) % NZ
        ref = gath.at[src_z * NYH + (yh if which == 0 else other), pl.ds(s0, n)]
        first = which == 0 and hop == 1 and not arriving
        return pltpu.make_async_remote_copy(
            src_ref=own.at[pl.ds(s0, n)] if first else ref,
            dst_ref=ref,
            send_sem=ring_send.at[direction, which, hop - 1, chunk],
            recv_sem=ring_recv.at[direction, which, hop - 1, chunk],
            device_id={"z": (z + sign + NZ) % NZ},
            device_id_type=MESH,
        )

    def across(far, chunk, arriving=False):
        s0, n = chunks[chunk]
        src_z = (z + 4) % NZ if far else z
        ref = gath.at[src_z * NYH + (other if arriving else yh), pl.ds(s0, n)]
        return pltpu.make_async_remote_copy(
            src_ref=ref if far or arriving else own.at[pl.ds(s0, n)],
            dst_ref=ref,
            send_sem=y_send.at[1 if far else 0, chunk],
            recv_sem=y_recv.at[1 if far else 0, chunk],
            device_id={"yh": other},
            device_id_type=MESH,
        )

    count = range(len(chunks))

    def launch(chunk):
        go(ring(0, 0, 1, chunk))
        go(ring(1, 0, 1, chunk))

    for g in count:
        design(g)

    for q in range(NCOL):
        at, found = jnp.int32(0), jnp.int32(0)
        for s in range(slots):
            hit = held[s] == base + q
            at = jnp.where(hit, s, at)
            found = jnp.where(hit, 1, found)
        got = jnp.where(found == 1, own[at].astype(jnp.float32), 0.0).astype(jnp.bfloat16)
        masked[pl.ds(2 * q, 2)] = got.reshape(2, 16, TILE)

    def ring_round(which, hop):
        for g in count:
            for direction in (0, 1):
                last = hops(which, g)[direction]
                if hop <= last:
                    ring(direction, which, hop, g, True).wait_recv()
                if hop < last:
                    go(ring(direction, which, hop + 1, g))
                if which == 0 and hop == 4 and hop == last:
                    go(across(True, g))

    def row_sends(stage, source, target):
        def send(i, c):
            k = (row + i) % NROW
            pltpu.make_async_remote_copy(
                src_ref=source(k),
                dst_ref=target,
                send_sem=c_send.at[stage],
                recv_sem=c_recv.at[stage],
                device_id=row_id(k),
                device_id_type=MESH,
            ).start()
            return c

        lax.fori_loop(1, NROW, send, 0)

    def row_wait(stage, buffer):
        lines = buffer.at[pl.ds(0, NROW - 1)]
        pltpu.make_async_copy(lines, lines, c_recv.at[stage]).wait()
        pltpu.make_async_copy(lines, lines, c_send.at[stage]).wait()

    def columns_out():
        row_sends(0, lambda k: masked.at[2 * met(k) + k % 2], parts.at[row])
        parts[row] = masked[2 * met(row) + half]

    cross = pltpu.make_async_remote_copy(
        src_ref=summed,
        dst_ref=column.at[row],
        send_sem=c_send.at[1],
        recv_sem=c_recv.at[1],
        device_id=facing,
        device_id_type=MESH,
    )

    def columns_added():
        row_wait(0, parts)
        total = parts[0].astype(jnp.float32)
        for k in range(1, NROW):
            total = total + parts[k].astype(jnp.float32)
        summed[...] = total.astype(jnp.bfloat16)

        @pl.when(away)
        def _():
            cross.start()

        @pl.when(jnp.logical_not(away))
        def _():
            column[row] = summed[...]

    def columns_spread():
        @pl.when(away)
        def _():
            cross.wait_send()
            pltpu.make_async_copy(column.at[row], column.at[row], c_recv.at[1]).wait()

        row_sends(2, lambda k: column.at[row], column.at[row])

    def columns_in():
        row_wait(2, column)
        for c in range(NCOL):
            k = ((c // NYH + z) % NZ) * 4 + ((c % NYH + yh) % NYH) * 2
            col = column[pl.ds(k, 2)].reshape(SHARD, TILE).astype(jnp.float32)
            value = col * wcol[c].reshape(SHARD, TILE)
            weighted[pl.ds(c * SHARD, SHARD)] = value.astype(jnp.bfloat16)

    def others_out():
        for g in count:
            across(False, g, True).wait_recv()
            go(ring(0, 1, 1, g))
            go(ring(1, 1, 1, g))

    pl.semaphore_wait(barrier, 3 + (NROW - 1) + jnp.where(away, 1, 0))
    for g in count:
        launch(g)
    columns_out()
    for g in count:
        go(across(False, g))

    weights = jnp.zeros((4, TILE), jnp.float32)
    for g in range(8):
        weights = jnp.where(span_of[...] == g, span_w[g], weights)
    weights = obs_w[...] * weights * (0.25 / math.sqrt(OBS))
    for b in range(4):
        wide = jnp.broadcast_to(weights[b : b + 1, :], (TILE, TILE))
        wcol[:, b] = jnp.transpose(wide).reshape(NCOL, 8, TILE)
    gath[mine] = own[...]

    steps = {
        "added": columns_added,
        "spread": columns_spread,
        "in": columns_in,
        "others": others_out,
    }
    for step in plan_of(slots):
        if step in steps:
            steps[step]()
        else:
            ring_round(*step)

    target = base + mine
    goal = packed if compact else prod
    weight_block = weighted[...]
    for g in count:
        ring(0, 1, 3, g, True).wait_recv()
        ring(1, 1, 3, g, True).wait_recv()
        across(True, g, True).wait_recv()
        s0, n = chunks[g]
        for k in range(s0, s0 + n):
            product = lax.dot_general(
                gath[:, k].reshape(OBS, TILE),
                weight_block,
                (((0,), (0,)), ((), ())),
                preferred_element_type=jnp.float32,
            )
            goal[k] = product if compact else jnp.where(tiles[k] >= target, product, 0.0)
    if compact:
        for s in range(SLOTS):
            keep = (place[s] >= 0) & (tiles[s] >= target)
            prod[s] = jnp.where(keep, packed[jnp.clip(place[s], 0, slots - 1)], 0.0)
    for copy in started:
        copy.wait_send()


def product_of(slots, identity):
    hbm = pl.BlockSpec(memory_space=pltpu.HBM)
    bf16, f32, i32 = jnp.bfloat16, jnp.float32, jnp.int32
    dma = pltpu.SemaphoreType.DMA
    pieces = len(chunks_of(slots))
    return pl.pallas_call(
        functools.partial(kernel, slots),
        out_shape=jax.ShapeDtypeStruct((SLOTS, TILE, TILE), f32),
        in_specs=[hbm] * 7,
        out_specs=pl.BlockSpec(memory_space=pltpu.VMEM),
        scratch_shapes=[
            pltpu.VMEM((4, SLOTS, 8, TILE), bf16),
            pltpu.SMEM((OBS,), f32),
            pltpu.VMEM((4, TILE), f32),
            pltpu.SMEM((8,), f32),
            pltpu.VMEM((4, TILE), i32),
            pltpu.SMEM((SLOTS * NROW,), i32),
            pltpu.SMEM((1,), i32),
            pltpu.VMEM((4, SHARD, TILE), f32),
            pltpu.VMEM((slots, SHARD, TILE), bf16),
            pltpu.VMEM((NCOL, slots, SHARD, TILE), bf16),
            pltpu.VMEM((NROW, 16, TILE), bf16),
            pltpu.VMEM((NROW, 16, TILE), bf16),
            pltpu.VMEM((16, TILE), bf16),
            pltpu.VMEM((NROW, 16, TILE), bf16),
            pltpu.VMEM((OBS, TILE), bf16),
            pltpu.VMEM((NCOL, 4, 8, TILE), f32),
            pltpu.VMEM((slots, TILE, TILE), f32),
            dma((7,)),
            dma((2, 2, 4, pieces)),
            dma((2, 2, 4, pieces)),
            dma((2, pieces)),
            dma((2, pieces)),
            dma((3,)),
            dma((3,)),
        ],
        compiler_params=pltpu.CompilerParams(
            collective_id=identity, has_side_effects=True, vmem_limit_bytes=24 * 1024 * 1024
        ),
    )


def per_device(
    legendre, longitude, obs_weight, span_weight, span_of, tile_order, slab_start, resident
):
    leg = legendre.reshape(4, 8, SLOTS, TILE).transpose(0, 2, 1, 3)
    given = (
        leg,
        longitude,
        obs_weight.reshape(4, TILE),
        span_weight,
        span_of.reshape(4, TILE),
        tile_order,
        slab_start,
    )
    if len(SIZES) > 1:
        reached = (tile_order >= slab_start) & (tile_order < TILES)
        counts = jnp.sum(reached.reshape(SLOTS, NROW).astype(jnp.int32), axis=0)
        level = jnp.max(sum((counts > size).astype(jnp.int32) for size in SIZES[:-1]))
        product = lax.switch(level, [product_of(size, i) for i, size in enumerate(SIZES)], *given)
    else:
        product = product_of(SIZES[0], 0)(*given)
    return resident + product.reshape(resident.shape)


def solution(mesh):
    torus = Mesh(
        mesh.devices.reshape(NX, NYL, NCORE, NZ, NYH), ("x", "yl", "core", "z", "yh")
    )
    rows, cols = ("x", "yl", "core"), ("z", "yh")
    return jax.shard_map(
        per_device,
        mesh=torus,
        in_specs=(
            P(None, cols, None, rows, None),
            P(),
            P(),
            P(),
            P(),
            P(),
            P(),
            P(None, rows, cols, None, None),
        ),
        out_specs=P(None, rows, cols, None, None),
        check_vma=False,
    )
```

time: 120 us -> 49.8 us (0.41); the launches traced: 119 us -> 50.7 us
  waiting for transfers between devices: 51.2 us -> 0 us
  Pallas kernels: 0 us -> 46.2 us
  blocking collectives: 31.7 us -> 0 us
  between operations: 16.8 us -> 1.33 us
  local copies, waits for them, and re-layouts: 6.84 us -> 0.08 us
  starting transfers between devices: 3.94 us -> 0 us
  matrix products: 3.53 us -> 0 us
  other arithmetic: 5.48 us -> 2.64 us
    all_gather x1 -> x0, waiting for transfers between devices: 47.4 us -> none  [gathered_by_axis(): nearer = lax.all_gather(array, axes[-1], axis=dim, tiled=True)]
    pallas_call x0 -> x1, Pallas kernels: none -> 46.2 us  [per_device(): lax.switch(level, [product_of(size, i) for i, size in enumerate(SIZES)],...]
    all_to_all x1 -> x0, blocking collectives: 17.2 us -> none  [sent_and_summed(): parts = lax.all_to_all(in_blocks(array, dim, count), axis, 0, 0, tiled=True)]
    all_gather x1 -> x0, blocking collectives: 14.5 us -> none  [gathered_by_axis(): nearer = lax.all_gather(array, axes[-1], axis=dim, tiled=True)]
    all_to_all x1 -> x0, starting transfers between devices: 3.91 us -> none  [copy_for_each(): lax.all_to_all(jnp.broadcast_to(array[None], (count, *array.shape)), axis...]
    all_to_all x1 -> x0, waiting for transfers between devices: 3.73 us -> none  [copy_for_each(): lax.all_to_all(jnp.broadcast_to(array[None], (count, *array.shape)), axis...]
    dot_general x1 -> x0, matrix products: 3.53 us -> none  [contract_rows(): lax.dot_general(left_side, right_side, (((0,), (0,)), ((), ())), preferre...]
    dot_general x1 -> x0, local copies, waits for them, and re-layouts: 3.42 us -> none  [contract_rows(): lax.dot_general(left_side, right_side, (((0,), (0,)), ((), ())), preferre...]
  transfers between devices with their start and end apart: 2 -> 0, of which waited for: 2 -> 0; matrix products, arithmetic and copies ran while one was open for 6% -> 0% of each run, Pallas kernels for 0% -> 0%
where the time goes in v2:
time: 49.8 us; the launch traced here: 50.7 us
  Pallas kernels  46.2 us (93%)
  other arithmetic  2.64 us (5%)
  between operations  1.33 us (3%)
    pallas_call x1, Pallas kernels, per_device(): lax.switch(level, [product_of(size, i) for i, size in enumerate(SIZES)],...  46.2 us
    add x1, other arithmetic, per_device(): return resident + product.reshape(resident.shape)  1.29 us

profile of v2, /device:TPU:1, one launch (start us, length us, event | category | flops | bytes accessed | tf_op | source)
XLA Modules:
  0.0 50.7 jit_solution(16339849664570921631)
XLA Ops:
  0.7 0.7 %and_convert_fusion = s32[736]{0:T(1024)S(1)} fusion(s32[736]{0:T(1024)} %param.18, s32[]{:T(128)} %bitcast.29), kind=kLoop, calls=%fused_computation | loop fusion | flops 2944 | bytes 5892 | tf_op jit(solution)/shard_map/convert_element_type | solution.py:429
  1.3 0.1 reshape.55
  1.4 0.6 %fusion.3 = s32[]{:T(128)} fusion(s32[32]{0:T(128)S(1)} %reduce_sum.9), kind=kLoop, calls=%fused_computation.8 | loop fusion | flops 383 | bytes 132 | tf_op jit(solution)/shard_map/reduce_max | solution.py:430
  2.7 0.0 copy-start
  2.7 46.6 %conditional.1 = (f32[23,1,1,128,128]{4,3,2,1,0:T(8,128)S(1)}) conditional(s32[]{:T(128)} %clamp.3, (f32[512]{0:T(512)}, s32[512]{0:T(512)}, bf16[4,23,8,128]{3,2,1,0:T(8,128)(2,1)}, f32[512]{0:T(512)}, f32[8]{0:T(128)}, /*index=5*/s32[736]{0:T(1024)}, s32[1]{0:T(128)}) %tuple.36, (f32[512]{0:T(512)}, s32[512]{0:T(512)}, ...), branch_computations={%region_2.0_spmd, %region_3.0_spmd, %region_4.0_spmd, %region_5.0_... | conditional | bytes 8 | solution.py:431
  2.8 46.2 %branch_3_fun.1 = f32[23,128,128]{2,1,0:T(8,128)S(1)} custom-call(bf16[4,23,8,128]{3,2,1,0:T(8,128)(2,1)} %get-tuple-element.113.leg_in, f32[512]{0:T(512)} %get-tuple-element.114.lon_in, f32[4,128]{1,0:T(4,128)} %bitcast.43, f32[8]{0:T(128)} %get-tuple-element.116.span_w_in, s32[4,128]{1,0:T(4,128)} %bitcast.48, s32[736]{0:T(1024)} %get-tuple-element.118.order_in, ...), custom_call_target="tpu_custom_call" | custom-call | tf_op jit(solution)/shard_map/cond/branch_3_fun/pallas_call | solution.py:431
  49.4 0.0 copy-done
  49.4 1.3 %add.15 = f32[23,1,1,128,128]{4,3,2,1,0:T(8,128)} add(f32[23,1,1,128,128]{4,3,2,1,0:T(8,128)S(1)} %copy-done, f32[23,1,1,128,128]{4,3,2,1,0:T(8,128)S(1)} %get-tuple-element.127) | non-fusion elementwise | flops 376832 | bytes 4521984 | tf_op jit(solution)/shard_map/add | solution.py:434
  (1 shorter events, 0.0 us)
Async XLA Ops:
  2.7 46.7 %copy-start = (f32[23,1,1,128,128]{4,3,2,1,0:T(8,128)S(1)}, f32[23,1,1,128,128]{4,3,2,1,0:T(8,128)}, u32[]{:S(2)}) copy-start(f32[23,1,1,128,128]{4,3,2,1,0:T(8,128)} %param.20) | copy-start | bytes 4521988

commit v3 on v2

--- a/solution.py
+++ b/solution.py
@@ -35,14 +35,10 @@
     return (4, 3) if chunk % 2 == 0 else (3, 4)
 
 
-def plan_of(slots):
-    if slots > 14:
-        return (
-            (0, 1), (0, 2), "added", (0, 3), "others", (0, 4), "spread", (1, 1), (1, 2), "in",
-        )
-    return (
-        (0, 1), (0, 2), "added", "others", (0, 3), (0, 4), (1, 1), "spread", (1, 2), "in",
-    )
+PLAN = (
+    (0, 1), "halfway", (0, 2), "added", (0, 3), "others", (0, 4), "spread", "far",
+    (1, 1), "across", (1, 2), "in",
+)
 
 
 def kernel(
@@ -67,6 +63,8 @@
     gath,
     masked,
     parts,
+    middle,
+    line,
     summed,
     column,
     weighted,
@@ -87,17 +85,18 @@
     row = (x * NYL + yl) * NCORE + core
     mine = z * NYH + yh
     other = 1 - yh
-    half = row % 2
-    facing_z, facing_y = (row // 4 - z + NZ) % NZ, (row // 2 + yh) % NYH
+    rank = (x * NCORE + core) * NYL + yl
+    lined = [({"yl": (yl + i) % NYL}, (yl + i) % NYL) for i in (2, 1, 3)]
+    crossed = []
+    for dx in (2, 1, 3, 0):
+        for dc in (1, 0):
+            if dx or dc:
+                to = {"x": (x + dx) % NX, "core": (core + dc) % NCORE}
+                crossed.append((to, to["x"] * NCORE + to["core"]))
+
+    facing_z, facing_y = (rank // 4 - z + NZ) % NZ, (rank // 2 + yh) % NYH
     away = (facing_z != z) | (facing_y != yh)
-
-    def row_id(k):
-        return {"x": k // (NYL * NCORE), "yl": (k // NCORE) % NYL, "core": k % NCORE}
-
     facing = {"z": facing_z, "yh": facing_y}
-
-    def met(k):
-        return ((k // 4 - z + NZ) % NZ) * NYH + (k // 2 + yh) % NYH
 
     inputs = []
     for i, (source, to) in enumerate(
@@ -120,10 +119,8 @@
     def hello(to):
         pl.semaphore_signal(barrier, inc=1, device_id=to, device_id_type=MESH)
 
-    def hello_row(i, c):
-        hello(row_id((row + i) % NROW))
-        return c
-
+    for to, _ in lined + crossed:
+        hello(to)
     hello({"z": (z + 1) % NZ})
     hello({"z": (z + NZ - 1) % NZ})
     hello({"yh": other})
@@ -131,8 +128,6 @@
     @pl.when(away)
     def _():
         hello(facing)
-
-    lax.fori_loop(1, NROW, hello_row, 0)
 
     for copy in inputs[:3]:
         copy.wait()
@@ -234,7 +229,8 @@
             at = jnp.where(hit, s, at)
             found = jnp.where(hit, 1, found)
         got = jnp.where(found == 1, own[at].astype(jnp.float32), 0.0).astype(jnp.bfloat16)
-        masked[pl.ds(2 * q, 2)] = got.reshape(2, 16, TILE)
+        k = ((q // NYH + z) % NZ) * 4 + ((q % NYH + yh) % NYH) * 2
+        masked[pl.ds(k, 2)] = got.reshape(2, 16, TILE)
 
     def ring_round(which, hop):
         for g in count:
@@ -244,48 +240,54 @@
                     ring(direction, which, hop, g, True).wait_recv()
                 if hop < last:
                     go(ring(direction, which, hop + 1, g))
-                if which == 0 and hop == 4 and hop == last:
-                    go(across(True, g))
-
-    def row_sends(stage, source, target):
-        def send(i, c):
-            k = (row + i) % NROW
+
+    def sends(stage, peers, source, target):
+        for to, k in peers:
             pltpu.make_async_remote_copy(
                 src_ref=source(k),
                 dst_ref=target,
                 send_sem=c_send.at[stage],
                 recv_sem=c_recv.at[stage],
-                device_id=row_id(k),
+                device_id=to,
                 device_id_type=MESH,
             ).start()
-            return c
-
-        lax.fori_loop(1, NROW, send, 0)
-
-    def row_wait(stage, buffer):
-        lines = buffer.at[pl.ds(0, NROW - 1)]
+
+    def arrived(stage, buffer, pieces):
+        lines = buffer.at[pl.ds(0, pieces)]
         pltpu.make_async_copy(lines, lines, c_recv.at[stage]).wait()
         pltpu.make_async_copy(lines, lines, c_send.at[stage]).wait()
 
+    def sum_of(values):
+        total = values[0].astype(jnp.float32)
+        for value in values[1:]:
+            total = total + value.astype(jnp.float32)
+        return total.astype(jnp.bfloat16)
+
+    block = pl.ds((x * NCORE + core) * NYL, NYL)
+
     def columns_out():
-        row_sends(0, lambda k: masked.at[2 * met(k) + k % 2], parts.at[row])
-        parts[row] = masked[2 * met(row) + half]
+        sends(0, crossed, lambda k: masked.at[pl.ds(k * NYL, NYL)], parts.at[block])
+        parts[block] = masked[block]
 
     cross = pltpu.make_async_remote_copy(
         src_ref=summed,
-        dst_ref=column.at[row],
-        send_sem=c_send.at[1],
-        recv_sem=c_recv.at[1],
+        dst_ref=column.at[rank],
+        send_sem=c_send.at[2],
+        recv_sem=c_recv.at[2],
         device_id=facing,
         device_id_type=MESH,
     )
 
+    def columns_halfway():
+        arrived(0, parts, 7 * NYL)
+        for j in range(NYL):
+            middle[j] = sum_of([parts[k * NYL + j] for k in range(NX * NCORE)])
+        sends(1, lined, lambda k: middle.at[k], line.at[yl])
+        line[yl] = middle[yl]
+
     def columns_added():
-        row_wait(0, parts)
-        total = parts[0].astype(jnp.float32)
-        for k in range(1, NROW):
-            total = total + parts[k].astype(jnp.float32)
-        summed[...] = total.astype(jnp.bfloat16)
+        arrived(1, line, NYL - 1)
+        summed[...] = sum_of([line[j] for j in range(NYL)])
 
         @pl.when(away)
         def _():
@@ -293,18 +295,22 @@
 
         @pl.when(jnp.logical_not(away))
         def _():
-            column[row] = summed[...]
+            column[rank] = summed[...]
 
     def columns_spread():
         @pl.when(away)
         def _():
             cross.wait_send()
-            pltpu.make_async_copy(column.at[row], column.at[row], c_recv.at[1]).wait()
-
-        row_sends(2, lambda k: column.at[row], column.at[row])
+            pltpu.make_async_copy(column.at[rank], column.at[rank], c_recv.at[2]).wait()
+
+        sends(3, lined, lambda k: column.at[rank], column.at[rank])
+
+    def columns_across():
+        arrived(3, line, NYL - 1)
+        sends(4, crossed, lambda k: column.at[block], column.at[block])
 
     def columns_in():
-        row_wait(2, column)
+        arrived(4, parts, 7 * NYL)
         for c in range(NCOL):
             k = ((c // NYH + z) % NZ) * 4 + ((c % NYH + yh) % NYH) * 2
             col = column[pl.ds(k, 2)].reshape(SHARD, TILE).astype(jnp.float32)
@@ -317,7 +323,11 @@
             go(ring(0, 1, 1, g))
             go(ring(1, 1, 1, g))
 
-    pl.semaphore_wait(barrier, 3 + (NROW - 1) + jnp.where(away, 1, 0))
+    def far_out():
+        for g in count:
+            go(across(True, g))
+
+    pl.semaphore_wait(barrier, 3 + len(lined + crossed) + jnp.where(away, 1, 0))
     for g in count:
         launch(g)
     columns_out()
@@ -334,12 +344,15 @@
     gath[mine] = own[...]
 
     steps = {
+        "halfway": columns_halfway,
         "added": columns_added,
+        "across": columns_across,
         "spread": columns_spread,
         "in": columns_in,
         "others": others_out,
+        "far": far_out,
     }
-    for step in plan_of(slots):
+    for step in PLAN:
         if step in steps:
             steps[step]()
         else:
@@ -392,6 +405,8 @@
             pltpu.VMEM((NCOL, slots, SHARD, TILE), bf16),
             pltpu.VMEM((NROW, 16, TILE), bf16),
             pltpu.VMEM((NROW, 16, TILE), bf16),
+            pltpu.VMEM((NYL, 16, TILE), bf16),
+            pltpu.VMEM((NYL, 16, TILE), bf16),
             pltpu.VMEM((16, TILE), bf16),
             pltpu.VMEM((NROW, 16, TILE), bf16),
             pltpu.VMEM((OBS, TILE), bf16),
@@ -402,8 +417,8 @@
             dma((2, 2, 4, pieces)),
             dma((2, pieces)),
             dma((2, pieces)),
-            dma((3,)),
-            dma((3,)),
+            dma((5,)),
+            dma((5,)),
         ],
         compiler_params=pltpu.CompilerParams(
             collective_id=identity, has_side_effects=True, vmem_limit_bytes=24 * 1024 * 1024

time: 49.8 us -> 47.3 us (0.950); the launches traced: 50.7 us -> 46.9 us
  Pallas kernels: 46.2 us -> 42.6 us
    pallas_call x1, Pallas kernels: 46.2 us -> 42.6 us  [per_device(): lax.switch(level, [product_of(size, i) for i, size in enumerate(SIZES)],...]
where the time goes in v3:
time: 47.3 us; the launch traced here: 46.9 us
  Pallas kernels  42.6 us (90%)
  other arithmetic  2.64 us (6%)
  between operations  1.33 us (3%)
    pallas_call x1, Pallas kernels, per_device(): lax.switch(level, [product_of(size, i) for i, size in enumerate(SIZES)],...  42.6 us
    add x1, other arithmetic, per_device(): return resident + product.reshape(resident.shape)  1.29 us

profile of v3, /device:TPU:1, one launch (start us, length us, event | category | flops | bytes accessed | tf_op | source)
XLA Modules:
  0.0 46.9 jit_solution(14872943063519743656)
XLA Ops:
  0.7 0.7 %and_convert_fusion = s32[736]{0:T(1024)S(1)} fusion(s32[736]{0:T(1024)} %param.18, s32[]{:T(128)} %bitcast.29), kind=kLoop, calls=%fused_computation | loop fusion | flops 2944 | bytes 5892 | tf_op jit(solution)/shard_map/convert_element_type | solution.py:444
  1.3 0.1 reshape.55
  1.4 0.6 %fusion.3 = s32[]{:T(128)} fusion(s32[32]{0:T(128)S(1)} %reduce_sum.9), kind=kLoop, calls=%fused_computation.8 | loop fusion | flops 383 | bytes 132 | tf_op jit(solution)/shard_map/reduce_max | solution.py:445
  2.7 0.0 copy-start
  2.7 42.8 %conditional.1 = (f32[23,1,1,128,128]{4,3,2,1,0:T(8,128)S(1)}) conditional(s32[]{:T(128)} %clamp.3, (f32[512]{0:T(512)}, s32[512]{0:T(512)}, bf16[4,23,8,128]{3,2,1,0:T(8,128)(2,1)}, f32[512]{0:T(512)}, f32[8]{0:T(128)}, /*index=5*/s32[736]{0:T(1024)}, s32[1]{0:T(128)}) %tuple.36, (f32[512]{0:T(512)}, s32[512]{0:T(512)}, ...), branch_computations={%region_2.0_spmd, %region_3.0_spmd, %region_4.0_spmd, %region_5.0_... | conditional | bytes 8 | solution.py:446
  2.8 42.6 %branch_1_fun.1 = f32[23,128,128]{2,1,0:T(8,128)S(1)} custom-call(bf16[4,23,8,128]{3,2,1,0:T(8,128)(2,1)} %get-tuple-element.99.leg_in, f32[512]{0:T(512)} %get-tuple-element.100.lon_in, f32[4,128]{1,0:T(4,128)} %bitcast.41, f32[8]{0:T(128)} %get-tuple-element.102.span_w_in, s32[4,128]{1,0:T(4,128)} %bitcast.46, s32[736]{0:T(1024)} %get-tuple-element.104.order_in, ...), custom_call_target="tpu_custom_call" | custom-call | tf_op jit(solution)/shard_map/cond/branch_1_fun/pallas_call | solution.py:446
  45.6 0.0 copy-done
  45.6 1.3 %add.15 = f32[23,1,1,128,128]{4,3,2,1,0:T(8,128)} add(f32[23,1,1,128,128]{4,3,2,1,0:T(8,128)S(1)} %copy-done, f32[23,1,1,128,128]{4,3,2,1,0:T(8,128)S(1)} %get-tuple-element.127) | non-fusion elementwise | flops 376832 | bytes 4521984 | tf_op jit(solution)/shard_map/add | solution.py:449
  (1 shorter events, 0.0 us)
Async XLA Ops:
  2.7 42.8 %copy-start = (f32[23,1,1,128,128]{4,3,2,1,0:T(8,128)S(1)}, f32[23,1,1,128,128]{4,3,2,1,0:T(8,128)}, u32[]{:S(2)}) copy-start(f32[23,1,1,128,128]{4,3,2,1,0:T(8,128)} %param.20) | copy-start | bytes 4521988
